TPU v7x, 32 devices: a whole 2x2x4 slice. The times are simulated.
32 devices in a mesh: tp: 4 (over y, x), grp: 8 (over z, core).
Axes of the slice: x: 2, y: 2, z: 4, core: 2. Of those that a mesh axis runs over, the one named last changes fastest.
Arguments:
- embeds: bfloat16 [2, 32, 8192], P(None, 'grp'), may hold values from -6 to 6
- ssm_state: bfloat16 [2, 32, 128, 64, 128], P(None, 'grp', 'tp'), may hold values from -2 to 2
- conv_state: bfloat16 [2, 32, 3, 8192], P(None, 'grp', None, 'tp'), may hold values from -6 to 6
- norm_gain: float32 [2, 8192], replicated, may hold values from 0.25 to 1.75
- in_weight: bfloat16 [2, 8192, 2, 8192], P(None, 'grp', None, 'tp'), may hold values from -0.0625 to 0.0625
- group_weight: bfloat16 [2, 8192, 384], P(None, 'grp'), may hold values from -0.03125 to 0.03125
- dt_bias: float32 [2, 128], P(None, 'tp'), may hold values from -2 to 1
- a_log: float32 [2, 128], P(None, 'tp'), may hold values from -1.5 to 1.5
- skip_gain: float32 [2, 128], P(None, 'tp'), may hold values from 0.5 to 1.5
- conv_weight: float32 [2, 4, 8192], P(None, None, 'tp'), may hold values from -3 to 3
- conv_bias: float32 [2, 8192], P(None, 'tp'), may hold values from -2 to 2
- out_weight: bfloat16 [2, 8192, 8192], P(None, 'tp', 'grp'), may hold values from -0.0625 to 0.0625
- leave_row: int32 [8], P('grp'), may hold values from 0 to 3
- arrive_from: int32 [8], P('grp'), may hold values from 0 to 7, as said below
Outputs:
- out_hidden: bfloat16 [2, 32, 8192], P(None, 'grp', 'tp')
Inputs may be any that keep to these rules, and one draw needn't show every extreme that they name: Every group appears exactly once in arrive_from: each group's leaving row fills exactly one freed slot.
All inputs are finite; a program needn't handle non-finite values.
Results may differ from a plain program's by a relative error of at most 0.02.
Values may be sent and summed in bfloat16 or wider, within the bound.
A program may use at most 128 MiB of HBM per device.

v0:
```python
import jax
import jax.numpy as jnp
from jax import lax
from jax.sharding import PartitionSpec as P


def local(
    embeds,
    ssm_state,
    conv_state,
    norm_gain,
    in_weight,
    group_weight,
    dt_bias,
    a_log,
    skip_gain,
    conv_weight,
    conv_bias,
    out_weight,
    leave_row,
    arrive_from,
):
    groups = lax.axis_size("grp")
    parts = lax.axis_size("tp")
    part_index = lax.axis_index("tp")
    steps = embeds.shape[0]
    row_dev = embeds.shape[1]
    model_width = embeds.shape[2]
    block_width = model_width // groups
    part_width = model_width // parts
    layers = ssm_state.shape[0]
    heads_dev = ssm_state.shape[2]
    head_dim = ssm_state.shape[3]
    state_dim = ssm_state.shape[4]
    channels = in_weight.shape[3]
    taps_count = conv_weight.shape[1]
    state_list = [ssm_state[i] for i in range(layers)]
    conv_list = [conv_state[i] for i in range(layers)]
    leaving = leave_row[0]
    anchor = arrive_from[0]

    def pick(carry, piece):
        count = piece[0].shape[0]
        hits = jnp.arange(count, dtype=jnp.int32) == anchor
        picked = []
        for total, member in zip(carry, piece):
            mask = hits.reshape((count,) + (1,) * (member.ndim - 1))
            picked.append(jnp.sum(jnp.where(mask, member, jnp.zeros_like(member)), axis=0))
        return tuple(picked)

    def leaving_rows():
        own_state = jnp.stack(
            [lax.dynamic_index_in_dim(s_arr, leaving, 0, False) for s_arr in state_list]
        )
        own_conv = jnp.stack(
            [lax.dynamic_index_in_dim(c_arr, leaving, 0, False) for c_arr in conv_list]
        )
        return (own_state, own_conv)

    def store_rows(got_state, got_conv):
        for i in range(layers):
            state_list[i] = lax.dynamic_update_index_in_dim(state_list[i], got_state[i], leaving, 0)
            conv_list[i] = lax.dynamic_update_index_in_dim(conv_list[i], got_conv[i], leaving, 0)

    def migrate_all():
        own_state, own_conv = leaving_rows()
        start_pair = (
            jnp.zeros(own_state.shape, jnp.bfloat16),
            jnp.zeros(own_conv.shape, jnp.bfloat16),
        )
        got_state, got_conv = pick(
            start_pair,
            (
                lax.all_gather(own_state[None], "grp", axis=0, tiled=True),
                lax.all_gather(own_conv[None], "grp", axis=0, tiled=True),
            ),
        )
        store_rows(got_state, got_conv)

    def migrate(layer):
        if layer == 0:
            migrate_all()

    def mixer(normed_block, layer):
        w_cols = in_weight[layer].reshape(block_width, 2 * channels)
        w_group = group_weight[layer]
        first = jnp.dot(normed_block, w_cols, preferred_element_type=jnp.float32)
        second = jnp.dot(normed_block, w_group, preferred_element_type=jnp.float32)
        summed = lax.psum_scatter(
            jnp.concatenate([first, second], axis=1), "grp", scatter_dimension=0, tiled=True
        )
        x_part = summed[:, :channels].astype(jnp.bfloat16)
        z_part = summed[:, channels : 2 * channels]
        b_mat = summed[:, 2 * channels : 2 * channels + state_dim]
        c_mat = summed[:, 2 * channels + state_dim : 2 * channels + 2 * state_dim]
        dt_all = summed[:, 2 * channels + 2 * state_dim :]
        dt_raw = lax.dynamic_slice_in_dim(dt_all, part_index * heads_dev, heads_dev, 1)
        taps = conv_weight[layer]
        window = conv_list[layer]
        conv_sum = x_part.astype(jnp.float32) * taps[taps_count - 1] + conv_bias[layer]
        for k in range(taps_count - 1):
            conv_sum = conv_sum + window[:, k].astype(jnp.float32) * taps[k]
        xc = jax.nn.silu(conv_sum)
        conv_list[layer] = jnp.concatenate([window[:, 1:], x_part[:, None, :]], axis=1)
        step_size = jax.nn.softplus(dt_raw + dt_bias[layer])
        decay = jnp.exp(-step_size * jnp.exp(a_log[layer]))
        xh = xc.reshape(row_dev, heads_dev, head_dim)
        fresh = (
            state_list[layer].astype(jnp.float32) * decay[:, :, None, None]
            + (step_size[:, :, None] * xh)[..., None] * b_mat[:, None, None, :]
        )
        state_list[layer] = fresh.astype(jnp.bfloat16)
        out_y = (
            jnp.sum(fresh * c_mat[:, None, None, :], axis=-1) + skip_gain[layer][None, :, None] * xh
        )
        gated = (out_y.reshape(row_dev, channels) * jax.nn.silu(z_part)).astype(jnp.bfloat16)
        w_back = out_weight[layer]
        partial_out = jnp.dot(
            lax.all_gather(gated, "grp", axis=0, tiled=True),
            w_back,
            preferred_element_type=jnp.float32,
        )
        return lax.psum(partial_out, "tp").astype(jnp.bfloat16)

    results = []
    for section in range(steps):
        carried = section > 0
        hidden = embeds[section]
        for layer in range(layers):
            if carried:
                migrate(layer)
            hf = hidden.astype(jnp.float32)
            normed = (
                hf * lax.rsqrt(jnp.mean(hf * hf, axis=-1, keepdims=True) + 1e-05) * norm_gain[layer]
            ).astype(jnp.bfloat16)
            normed_block = lax.all_to_all(normed, "grp", split_axis=1, concat_axis=0, tiled=True)
            delta = mixer(normed_block, layer)
            delta_rows = lax.all_to_all(delta, "grp", split_axis=0, concat_axis=1, tiled=True)
            hidden = (hf + delta_rows.astype(jnp.float32)).astype(jnp.bfloat16)
        results.append(lax.dynamic_slice_in_dim(hidden, part_index * part_width, part_width, 1))
    return jnp.stack(results)


def solution(mesh):
    placed = (
        P(None, "grp", None),
        P(None, "grp", "tp", None, None),
        P(None, "grp", None, "tp"),
        P(),
        P(None, "grp", None, "tp"),
        P(None, "grp", None),
        P(None, "tp"),
        P(None, "tp"),
        P(None, "tp"),
        P(None, None, "tp"),
        P(None, "tp"),
        P(None, "tp", "grp"),
        P("grp"),
        P("grp"),
    )
    return jax.shard_map(
        local, mesh=mesh, in_specs=placed, out_specs=P(None, "grp", "tp"), check_vma=False
    )
```

profile of v0, /device:TPU:0, one launch (start us, length us, event | category | flops | bytes accessed | tf_op | source)
XLA Modules:
  0.0 559.2 jit_solution(1863969251240788435)
XLA Ops:
  6.5 0.9 slice_convert_fusion.1
  7.4 1.1 fusion.32
  8.5 1.1 slice_reduce_fusion
  10.4 6.4 %all-to-all-start.4 = ((bf16[4,8,1024]{2,0,1:T(4,128)(2,1)}), bf16[4,8,1024]{2,0,1:T(4,128)(2,1)S(1)}, u32[]{:S(2)}, u32[]{:S(2)}) async-start(bf16[4,8,1024]{2,0,1:T(4,128)(2,1)} %get-tuple-element.60), calls=%async_computation.4 | async-start | bytes 131072 | tf_op jit(solution)/shard_map/all_to_all | solution.py:136
  16.8 14.3 %fusion.74 = (bf16[1,1024,2,2048]{3,2,1,0:T(2,128)(2,1)}, bf16[1,1024,2,2048]{3,2,1,0:T(2,128)(2,1)}) fusion(bf16[2,1024,2,2048]{3,2,1,0:T(2,128)(2,1)} %param.18), kind=kLoop, calls=%fused_computation.180 | loop fusion | bytes 33554432 | tf_op jit(solution)/shard_map/slice | solution.py:85
  31.1 12.1 %copy.33 = bf16[128,8,2,2048]{3,1,2,0:T(8,128)(2,1)} copy(bf16[128,8,2,2048]{3,2,1,0:T(2,128)(2,1)} %bitcast.216) | data formatting | bytes 16777216
  44.1 12.2 %copy.34 = bf16[128,8,2,2048]{3,1,2,0:T(8,128)(2,1)} copy(bf16[128,8,2,2048]{3,2,1,0:T(2,128)(2,1)} %bitcast.215) | data formatting | bytes 16777216
  57.5 5.1 all-to-all-start
  63.5 5.1 all-to-all-done
  68.8 4.9 fusion.82
  73.7 0.9 pad_maximum_fusion.1
  74.6 4.9 fusion.84
  79.5 50.4 %all-reduce.13.cloned.1.call-done = f32[32,4480]{1,0:T(8,128)} async-done(((f32[32,4480]{1,0:T(8,128)}), f32[32,4480]{1,0:T(8,128)}) %all-reduce.13.cloned.1.call-update) | async-done | bytes 573456
  130.0 0.9 divide_multiply_fusion.7
  131.0 0.9 fusion.78
  132.0 4.2 fusion.11
  136.3 1.0 fusion.62
  137.3 14.0 %all-gather.2 = bf16[8,4,2048]{2,1,0:T(4,128)(2,1)S(1)} all-gather(bf16[1,4,2048]{2,1,0:T(4,128)(2,1)S(1)} %fusion.62), channel_id=1, replica_groups=mesh['tp'=4,'grp'=8] {'grp'}, dimensions={0}, use_global_device_ids=true | all-gather | bytes 147456 | tf_op jit(solution)/shard_map/all_gather | solution.py:119
  152.0 3.1 fusion.8
  155.1 18.5 %all-reduce.18 = bf16[32,1024]{1,0:T(8,128)(2,1)S(1)} all-reduce(f32[32,1024]{1,0:T(8,128)S(1)} %fusion.8), channel_id=1, replica_groups=mesh['tp'=4,'grp'=8] {'tp'}, use_global_device_ids=true, to_apply=%region_3.4 | all-reduce | flops 32768 | bytes 196608 | tf_op jit(solution)/shard_map/psum | solution.py:123
  174.2 3.3 all-to-all-start.1
  177.6 1.3 fusion.20
  179.0 4.5 all-to-all-done.1
  184.4 3.3 all-to-all-start.2
  187.8 0.9 pad_maximum_fusion.3
  188.7 4.9 all-to-all-done.2
  193.6 1.3 fusion.18
  195.0 4.9 fusion.83
  199.9 0.8 pad_maximum_fusion.2
  201.6 55.8 %all-reduce.17.cloned.1.call-done = (f32[32,4480]{1,0:T(8,128)}, f32[32,4480]{1,0:T(8,128)}) async-done(((f32[32,4480]{1,0:T(8,128)}, f32[32,4480]{1,0:T(8,128)}), (f32[32,4480]{1,0:T(8,128)}, f32[32,4480]{1,0:T(8,128)})) %all-reduce.17.cloned.1.call-update) | async-done | bytes 1146896
  258.2 0.9 divide_multiply_fusion.5
  259.4 4.2 multiply_reduce_fusion.2
  263.6 1.3 copy-done
  265.0 1.1 pad_maximum_fusion
  266.9 0.9 fusion.66
  267.8 0.9 fusion.67
  268.8 15.4 %all-gather.1 = bf16[16,3,2048]{2,1,0:T(4,128)(2,1)S(1)} all-gather(bf16[2,3,2048]{2,1,0:T(4,128)(2,1)S(1)} %copy.29), channel_id=3, replica_groups=mesh['tp'=4,'grp'=8] {'grp'}, dimensions={0}, use_global_device_ids=true | all-gather | bytes 221184 | tf_op jit(solution)/shard_map/all_gather | solution.py:75
  284.8 0.9 divide_multiply_fusion.3
  285.8 0.8 fusion.77
  286.8 61.5 %all-gather.8.cloned.1.call-done = bf16[16,32,64,128]{3,2,1,0:T(8,128)(2,1)} async-done(((bf16[2,32,64,128]{3,2,1,0:T(8,128)(2,1)}), bf16[16,32,64,128]{3,2,1,0:T(8,128)(2,1)}) %all-gather.8.cloned.1.call-update) | async-done | bytes 8388624 | tf_op jit(solution)/shard_map/all_gather | solution.py:74
  348.3 5.6 select_reduce_fusion
  353.9 0.9 slice_dynamic-update-slice_fusion
  354.8 2.8 multiply_reduce_fusion.1
  357.8 1.1 fusion.64
  358.9 14.0 %all-gather.4 = bf16[8,4,2048]{2,1,0:T(4,128)(2,1)S(1)} all-gather(bf16[1,4,2048]{2,1,0:T(4,128)(2,1)S(1)} %fusion.64), channel_id=1, replica_groups=mesh['tp'=4,'grp'=8] {'grp'}, dimensions={0}, use_global_device_ids=true | all-gather | bytes 147456 | tf_op jit(solution)/shard_map/all_gather | solution.py:119
  372.9 3.0 fusion.6
  375.9 18.5 %all-reduce.19 = bf16[32,1024]{1,0:T(8,128)(2,1)S(1)} all-reduce(f32[32,1024]{1,0:T(8,128)S(1)} %fusion.6), channel_id=1, replica_groups=mesh['tp'=4,'grp'=8] {'tp'}, use_global_device_ids=true, to_apply=%region_13.14 | all-reduce | flops 32768 | bytes 196608 | tf_op jit(solution)/shard_map/psum | solution.py:123
  394.4 8.3 %all_to_all.116 = bf16[8,4,1024]{2,1,0:T(4,128)(2,1)S(1)} all-to-all(bf16[8,4,1024]{2,1,0:T(4,128)(2,1)S(1)} %all_to_all.101), channel_id=1, replica_groups=mesh['tp'=4,'grp'=8] {'grp'}, dimensions={0} | all-to-all | bytes 131072 | tf_op jit(solution)/shard_map/all_to_all | solution.py:138
  403.0 8.3 %all_to_all.117 = bf16[4,8,1024]{2,0,1:T(4,128)(2,1)S(1)} all-to-all(bf16[4,8,1024]{2,0,1:T(4,128)(2,1)S(1)} %multiply_convert_fusion), channel_id=1, replica_groups=mesh['tp'=4,'grp'=8] {'grp'}, dimensions={1} | all-to-all | bytes 131072 | tf_op jit(solution)/shard_map/all_to_all | solution.py:136
  411.6 5.1 fusion.85
  416.7 0.9 pad_maximum_fusion.4
  418.1 53.1 %all-reduce.15.cloned.1.call-done = f32[32,4480]{1,0:T(8,128)} async-done(((f32[32,4480]{1,0:T(8,128)}), f32[32,4480]{1,0:T(8,128)}) %all-reduce.15.cloned.1.call-update) | async-done | bytes 573456
  471.2 0.9 divide_multiply_fusion.1
  473.2 2.9 multiply_reduce_fusion
  476.2 1.0 fusion.63
  477.2 14.0 %all-gather.5 = bf16[8,4,2048]{2,1,0:T(4,128)(2,1)S(1)} all-gather(bf16[1,4,2048]{2,1,0:T(4,128)(2,1)S(1)} %get-tuple-element.64), channel_id=1, replica_groups=mesh['tp'=4,'grp'=8] {'grp'}, dimensions={0}, use_global_device_ids=true | all-gather | bytes 147456 | tf_op jit(solution)/shard_map/all_gather | solution.py:119
  491.2 3.0 fusion.2
  494.3 14.0 %all-gather.3 = bf16[8,4,2048]{2,1,0:T(4,128)(2,1)S(1)} all-gather(bf16[1,4,2048]{2,1,0:T(4,128)(2,1)S(1)} %get-tuple-element.63), channel_id=1, replica_groups=mesh['tp'=4,'grp'=8] {'grp'}, dimensions={0}, use_global_device_ids=true | all-gather | bytes 147456 | tf_op jit(solution)/shard_map/all_gather | solution.py:119
  508.3 3.0 fusion.4
  511.3 21.7 %all-reduce.20 = (bf16[32,1024]{1,0:T(8,128)(2,1)S(1)}, bf16[32,1024]{1,0:T(8,128)(2,1)S(1)}) all-reduce(f32[32,1024]{1,0:T(8,128)S(1)} %fusion.2, f32[32,1024]{1,0:T(8,128)S(1)} %fusion.4), channel_id=1, replica_groups=mesh['tp'=4,'grp'=8] {'tp'}, use_global_device_ids=true, to_apply=%region_17.18 | all-reduce | flops 65536 | bytes 393216 | tf_op jit(solution)/shard_map/psum | solution.py:123
  533.6 3.3 all-to-all-start.7
  537.6 5.2 all-to-all-done.7
  542.8 3.3 all-to-all-start.3
  546.2 5.8 %all-to-all-done.3 = bf16[8,4,1024]{2,1,0:T(4,128)(2,1)S(1)} async-done(((bf16[8,4,1024]{2,1,0:T(4,128)(2,1)}), bf16[8,4,1024]{2,1,0:T(4,128)(2,1)S(1)}, u32[]{:S(2)}, u32[]{:S(2)}) %all-to-all-start.3) | async-done | bytes 65568 | tf_op jit(solution)/shard_map/all_to_all | solution.py:138
  (130 shorter events, 13.0 us)
Async XLA Ops:
  10.4 47.1 %all-to-all-start.4 = ((bf16[4,8,1024]{2,0,1:T(4,128)(2,1)}), bf16[4,8,1024]{2,0,1:T(4,128)(2,1)S(1)}, u32[]{:S(2)}, u32[]{:S(2)}) async-start(bf16[4,8,1024]{2,0,1:T(4,128)(2,1)} %get-tuple-element.60), calls=%async_computation.4 | async-start | bytes 131072 | tf_op jit(solution)/shard_map/all_to_all | solution.py:136
  31.0 12.1 %copy-start.5 = (bf16[2,4,3,2048]{3,1,2,0:T(4,128)(2,1)S(1)}, bf16[2,4,3,2048]{3,1,2,0:T(4,128)(2,1)}, u32[]{:S(2)}) copy-start(bf16[2,4,3,2048]{3,1,2,0:T(4,128)(2,1)} %param.16) | copy-start | bytes 294916
  31.1 12.2 %copy-start.8 = (f32[2,4,2048]{2,1,0:T(4,128)S(1)}, f32[2,4,2048]{2,1,0:T(4,128)}, u32[]{:S(2)}) copy-start(f32[2,4,2048]{2,1,0:T(4,128)} %param.23) | copy-start | bytes 196612
  31.1 12.2 %copy-start.9 = (f32[2,2048]{1,0:T(2,128)S(1)}, f32[2,2048]{1,0:T(2,128)}, u32[]{:S(2)}) copy-start(f32[2,2048]{1,0:T(2,128)} %param.24) | copy-start | bytes 49156
  31.1 12.3 %copy-start.19 = (f32[2,32]{1,0:T(2,128)S(1)}, f32[2,32]{1,0:T(2,128)}, u32[]{:S(2)}) copy-start(f32[2,32]{1,0:T(2,128)} %param.22) | copy-start | bytes 772
  44.1 92.3 %copy-start.6 = (f32[2048]{0:T(1024)}, f32[2048]{0:T(1024)S(1)}, u32[]{:S(2)}) copy-start(f32[2048]{0:T(1024)S(1)} %mul.533) | copy-start | bytes 24580
  44.1 12.2 %copy-start.22 = (u32[32]{0:T(128)S(1)}, u32[32]{0:T(128)}, u32[]{:S(2)}) copy-start(u32[32]{0:T(128)} %constant.77) | copy-start | bytes 388
  44.1 18.8 %copy-start.20 = (f32[2,32]{1,0:T(2,128)S(1)}, f32[2,32]{1,0:T(2,128)}, u32[]{:S(2)}) copy-start(f32[2,32]{1,0:T(2,128)} %param.21) | copy-start | bytes 772
  44.1 18.8 %copy-start.21 = (f32[2,32]{1,0:T(2,128)S(1)}, f32[2,32]{1,0:T(2,128)}, u32[]{:S(2)}) copy-start(f32[2,32]{1,0:T(2,128)} %param.20) | copy-start | bytes 772
  44.1 24.5 %copy-start.2 = (bf16[2,1024,384]{2,1,0:T(8,128)(2,1)S(1)}, bf16[2,1024,384]{2,1,0:T(8,128)(2,1)}, u32[]{:S(2)}) copy-start(bf16[2,1024,384]{2,1,0:T(8,128)(2,1)} %param.19) | copy-start | bytes 4718596
  57.5 11.0 %all-to-all-start = ((bf16[4,8,1024]{2,0,1:T(4,128)(2,1)}), bf16[4,8,1024]{2,0,1:T(4,128)(2,1)S(1)}, u32[]{:S(2)}, u32[]{:S(2)}) async-start(bf16[4,8,1024]{2,0,1:T(4,128)(2,1)} %get-tuple-element.59), calls=%async_computation | async-start | bytes 131072 | tf_op jit(solution)/shard_map/all_to_all | solution.py:136
  62.6 67.3 %all-reduce.13.cloned.1.call-start = ((), (), s32[]{:S(2)}) async-start(), calls=%async_computation.9 | async-start | bytes 1146880
  63.5 68.4 %copy-start.14 = (f32[32]{0:T(128)}, f32[32]{0:T(128)S(1)}, u32[]{:S(2)}) copy-start(f32[32]{0:T(128)S(1)} %get-tuple-element.70) | copy-start | bytes 388
  63.5 68.4 %copy-start.16 = (f32[32]{0:T(128)}, f32[32]{0:T(128)S(1)}, u32[]{:S(2)}) copy-start(f32[32]{0:T(128)S(1)} %get-tuple-element.73) | copy-start | bytes 388
  136.2 47.2 %copy-start.4 = (bf16[2,4,8192]{2,1,0:T(4,128)(2,1)S(1)}, bf16[2,4,8192]{2,1,0:T(4,128)(2,1)}, u32[]{:S(2)}) copy-start(bf16[2,4,8192]{2,1,0:T(4,128)(2,1)} %param.14) | copy-start | bytes 393220
  174.2 9.2 %all-to-all-start.1 = ((bf16[8,4,1024]{2,1,0:T(4,128)(2,1)}), bf16[8,4,1024]{2,1,0:T(4,128)(2,1)S(1)}, u32[]{:S(2)}, u32[]{:S(2)}) async-start(bf16[8,4,1024]{2,1,0:T(4,128)(2,1)} %all_to_all.91), calls=%async_computation.1 | async-start | bytes 131072 | tf_op jit(solution)/shard_map/all_to_all | solution.py:138
  184.4 9.2 %all-to-all-start.2 = ((bf16[4,8,1024]{2,0,1:T(4,128)(2,1)}), bf16[4,8,1024]{2,0,1:T(4,128)(2,1)S(1)}, u32[]{:S(2)}, u32[]{:S(2)}) async-start(bf16[4,8,1024]{2,0,1:T(4,128)(2,1)} %multiply_convert_fusion.2), calls=%async_computation.2 | async-start | bytes 131072 | tf_op jit(solution)/shard_map/all_to_all | solution.py:136
  187.8 69.6 %all-reduce.17.cloned.1.call-start = ((), (), s32[]{:S(2)}) async-start(), calls=%async_computation.11 | async-start | bytes 2293760
  195.0 64.2 %copy-start.10 = (f32[32]{0:T(128)S(1)}, f32[32]{0:T(128)}, u32[]{:S(2)}) copy-start(f32[32]{0:T(128)} %get-tuple-element.69) | copy-start | bytes 388
  195.0 64.2 %copy-start.12 = (f32[32]{0:T(128)S(1)}, f32[32]{0:T(128)}, u32[]{:S(2)}) copy-start(f32[32]{0:T(128)} %get-tuple-element.74) | copy-start | bytes 388
  200.8 147.5 %all-gather.8.cloned.1.call-start = ((), (), s32[]{:S(2)}) async-start(), calls=%async_computation.8 | async-start | bytes 9437184 | tf_op jit(solution)/shard_map/all_gather | solution.py:74
  259.4 27.2 %copy-start.15 = (f32[32]{0:T(128)S(1)}, f32[32]{0:T(128)}, u32[]{:S(2)}) copy-start(f32[32]{0:T(128)} %copy-done.14) | copy-start | bytes 388
  259.4 27.2 %copy-start.17 = (f32[32]{0:T(128)S(1)}, f32[32]{0:T(128)}, u32[]{:S(2)}) copy-start(f32[32]{0:T(128)} %copy-done.16) | copy-start | bytes 388
  263.6 1.3 copy-start
  266.1 205.1 %all-reduce.15.cloned.1.call-start = ((), (), s32[]{:S(2)}) async-start(), calls=%async_computation.10 | async-start | bytes 1146880
  353.9 3.8 copy-start.7
  357.7 53.7 %copy-start.3 = (bf16[2,1024,384]{2,1,0:T(8,128)(2,1)S(1)}, bf16[2,1024,384]{2,1,0:T(8,128)(2,1)}, u32[]{:S(2)}) copy-start(bf16[2,1024,384]{2,1,0:T(8,128)(2,1)} %param.19) | copy-start | bytes 4718596
  411.6 6.0 %copy-start.18 = (f32[32]{0:T(128)S(1)}, f32[32]{0:T(128)}, u32[]{:S(2)}) copy-start(f32[32]{0:T(128)} %get-tuple-element.65) | copy-start | bytes 388
  411.6 61.4 %copy-start.11 = (f32[32]{0:T(128)S(1)}, f32[32]{0:T(128)}, u32[]{:S(2)}) copy-start(f32[32]{0:T(128)} %get-tuple-element.69) | copy-start | bytes 388
  411.6 61.4 %copy-start.13 = (f32[32]{0:T(128)S(1)}, f32[32]{0:T(128)}, u32[]{:S(2)}) copy-start(f32[32]{0:T(128)} %get-tuple-element.74) | copy-start | bytes 388
  411.6 61.6 %copy-start.1 = (bf16[4,32,64,128]{3,2,1,0:T(8,128)(2,1)S(1)}, bf16[4,32,64,128]{3,2,1,0:T(8,128)(2,1)}, u32[]{:S(2)}) copy-start(bf16[4,32,64,128]{3,2,1,0:T(8,128)(2,1)} %get-tuple-element.31) | copy-start | bytes 6291460
  533.6 9.2 %all-to-all-start.7 = ((bf16[8,4,1024]{2,1,0:T(4,128)(2,1)}), bf16[8,4,1024]{2,1,0:T(4,128)(2,1)S(1)}, u32[]{:S(2)}, u32[]{:S(2)}) async-start(bf16[8,4,1024]{2,1,0:T(4,128)(2,1)} %all_to_all.106), calls=%async_computation.7 | async-start | bytes 131072 | tf_op jit(solution)/shard_map/all_to_all | solution.py:138
  542.8 9.2 %all-to-all-start.3 = ((bf16[8,4,1024]{2,1,0:T(4,128)(2,1)}), bf16[8,4,1024]{2,1,0:T(4,128)(2,1)S(1)}, u32[]{:S(2)}, u32[]{:S(2)}) async-start(bf16[8,4,1024]{2,1,0:T(4,128)(2,1)} %all_to_all.96), calls=%async_computation.3 | async-start | bytes 131072 | tf_op jit(solution)/shard_map/all_to_all | solution.py:138
Sparse Core Ops, SparseCore 0:
  74.7 55.1 all-reduce.12
  200.9 56.3 all-reduce.16
  266.2 82.0 all-gather.7
  417.7 53.4 all-reduce.14
where the time goes:
time: 561 us; the launch traced here: 559 us
  waiting for transfers between devices  246 us (44%)
  blocking collectives  146 us (26%)
  local copies, waits for them, and re-layouts  53.6 us (10%)
  other arithmetic  36.8 us (7%)
  matrix products  35.1 us (6%)
  starting transfers between devices  25.2 us (4%)
  between operations  15.8 us (3%)
    unnamed x7, waiting for transfers between devices  159 us
    all_gather x1, waiting for transfers between devices, migrate_all(): lax.all_gather(own_state[None], 'grp', axis=0, tiled=True)  61.5 us
    psum x3, blocking collectives, mixer(): return lax.psum(partial_out, 'tp').astype(jnp.bfloat16)  58.6 us
    all_gather x4, blocking collectives, mixer(): lax.all_gather(gated, 'grp', axis=0, tiled=True)  55.9 us
    unnamed x53, local copies, waits for them, and re-layouts  27 us
    dot_general x4, matrix products, mixer(): first = jnp.dot(normed_block, w_cols, preferred_element_type=jnp.float32)  19.9 us
    all_to_all x3, waiting for transfers between devices, local(): lax.all_to_all(delta, 'grp', split_axis=0, concat_axis=1, tiled=True)  15.5 us
    all_gather x1, blocking collectives, migrate_all(): lax.all_gather(own_conv[None], 'grp', axis=0, tiled=True)  15.4 us
  transfers between devices with their start and end apart: 10, of which 9 were waited for; matrix products, arithmetic and copies ran while one was open for 9% of the time, Pallas kernels for 0%

commit v1 on v0

--- a/solution.py
+++ b/solution.py
@@ -135,7 +135,9 @@
             ).astype(jnp.bfloat16)
             normed_block = lax.all_to_all(normed, "grp", split_axis=1, concat_axis=0, tiled=True)
             delta = mixer(normed_block, layer)
-            delta_rows = lax.all_to_all(delta, "grp", split_axis=0, concat_axis=1, tiled=True)
+            pieces = jnp.split(delta, lax.axis_size("grp"), axis=0)
+            incoming = lax.all_to_all(jnp.stack(pieces), "grp", 0, 0)
+            delta_rows = jnp.concatenate(incoming, axis=1)
             hidden = (hf + delta_rows.astype(jnp.float32)).astype(jnp.bfloat16)
         results.append(lax.dynamic_slice_in_dim(hidden, part_index * part_width, part_width, 1))
     return jnp.stack(results)

time: 561 us -> 570 us (1.016)
  local copies, waits for them, and re-layouts: 53.6 us -> 66.1 us
    unnamed x53 -> x81, local copies, waits for them, and re-layouts: 27 us -> 39.7 us
  transfers between devices with their start and end apart: 10 -> 10, of which waited for: 9 -> 9; matrix products, arithmetic and copies ran while one was open for 9% -> 10% of each run, Pallas kernels for 0% -> 0%
where the time goes in v1:
time: 570 us; the launch traced here: 568 us
  waiting for transfers between devices  242 us (42%)
  blocking collectives  146 us (26%)
  local copies, waits for them, and re-layouts  66.1 us (12%)
  other arithmetic  36.8 us (6%)
  matrix products  35.1 us (6%)
  starting transfers between devices  25.8 us (5%)
  between operations  15.8 us (3%)
    unnamed x7, waiting for transfers between devices  159 us
    all_gather x1, waiting for transfers between devices, migrate_all(): lax.all_gather(own_state[None], 'grp', axis=0, tiled=True)  61.5 us
    psum x3, blocking collectives, mixer(): return lax.psum(partial_out, 'tp').astype(jnp.bfloat16)  58.6 us
    all_gather x4, blocking collectives, mixer(): lax.all_gather(gated, 'grp', axis=0, tiled=True)  55.9 us
    unnamed x81, local copies, waits for them, and re-layouts  39.7 us
    dot_general x4, matrix products, mixer(): first = jnp.dot(normed_block, w_cols, preferred_element_type=jnp.float32)  19.9 us
    all_gather x1, blocking collectives, migrate_all(): lax.all_gather(own_conv[None], 'grp', axis=0, tiled=True)  15.4 us
    all_to_all x3, starting transfers between devices, local(): lax.all_to_all(normed, 'grp', split_axis=1, concat_axis=0, tiled=True)  14.8 us
  transfers between devices with their start and end apart: 10, of which 9 were waited for; matrix products, arithmetic and copies ran while one was open for 10% of the time, Pallas kernels for 0%

profile of v1, /device:TPU:0, one launch (start us, length us, event | category | flops | bytes accessed | tf_op | source)
XLA Modules:
  0.0 568.3 jit_solution(8583019725025389359)
XLA Ops:
  6.5 0.9 slice_convert_fusion.1
  7.4 1.1 fusion.32
  8.5 1.1 slice_reduce_fusion
  10.4 6.4 %all-to-all-start.4 = ((bf16[4,8,1024]{2,0,1:T(4,128)(2,1)}), bf16[4,8,1024]{2,0,1:T(4,128)(2,1)S(1)}, u32[]{:S(2)}, u32[]{:S(2)}) async-start(bf16[4,8,1024]{2,0,1:T(4,128)(2,1)} %get-tuple-element.60), calls=%async_computation.4 | async-start | bytes 131072 | tf_op jit(solution)/shard_map/all_to_all | solution.py:136
  16.8 14.3 %fusion.74 = (bf16[1,1024,2,2048]{3,2,1,0:T(2,128)(2,1)}, bf16[1,1024,2,2048]{3,2,1,0:T(2,128)(2,1)}) fusion(bf16[2,1024,2,2048]{3,2,1,0:T(2,128)(2,1)} %param.18), kind=kLoop, calls=%fused_computation.244 | loop fusion | bytes 33554432 | tf_op jit(solution)/shard_map/slice | solution.py:85
  31.1 12.1 %copy.19 = bf16[128,8,2,2048]{3,1,2,0:T(8,128)(2,1)} copy(bf16[128,8,2,2048]{3,2,1,0:T(2,128)(2,1)} %bitcast.342) | data formatting | bytes 16777216
  44.1 12.2 %copy.20 = bf16[128,8,2,2048]{3,1,2,0:T(8,128)(2,1)} copy(bf16[128,8,2,2048]{3,2,1,0:T(2,128)(2,1)} %bitcast.341) | data formatting | bytes 16777216
  57.5 5.1 all-to-all-start
  63.5 5.1 all-to-all-done
  68.8 4.9 fusion.82
  73.7 0.9 pad_maximum_fusion.1
  74.6 4.9 fusion.84
  79.5 50.4 %all-reduce.13.cloned.1.call-done = f32[32,4480]{1,0:T(8,128)} async-done(((f32[32,4480]{1,0:T(8,128)}), f32[32,4480]{1,0:T(8,128)}) %all-reduce.13.cloned.1.call-update) | async-done | bytes 573456
  130.0 0.9 divide_multiply_fusion.7
  132.0 4.2 fusion.11
  136.3 1.0 fusion.62
  137.3 14.0 %all-gather.2 = bf16[8,4,2048]{2,1,0:T(4,128)(2,1)S(1)} all-gather(bf16[1,4,2048]{2,1,0:T(4,128)(2,1)S(1)} %fusion.62), channel_id=1, replica_groups=mesh['tp'=4,'grp'=8] {'grp'}, dimensions={0}, use_global_device_ids=true | all-gather | bytes 147456 | tf_op jit(solution)/shard_map/all_gather | solution.py:119
  152.0 3.1 fusion.8
  155.1 18.5 %all-reduce.18 = bf16[32,1024]{1,0:T(8,128)(2,1)S(1)} all-reduce(f32[32,1024]{1,0:T(8,128)S(1)} %fusion.8), channel_id=1, replica_groups=mesh['tp'=4,'grp'=8] {'tp'}, use_global_device_ids=true, to_apply=%region_3.4 | all-reduce | flops 32768 | bytes 196608 | tf_op jit(solution)/shard_map/psum | solution.py:123
  178.4 3.3 all-to-all-start.1
  181.7 1.3 fusion.20
  183.1 4.5 all-to-all-done.1
  188.5 3.3 all-to-all-start.2
  191.9 0.9 pad_maximum_fusion.3
  192.8 4.9 all-to-all-done.2
  197.8 1.3 fusion.18
  199.1 4.9 fusion.83
  204.1 0.8 pad_maximum_fusion.2
  205.7 55.8 %all-reduce.17.cloned.1.call-done = (f32[32,4480]{1,0:T(8,128)}, f32[32,4480]{1,0:T(8,128)}) async-done(((f32[32,4480]{1,0:T(8,128)}, f32[32,4480]{1,0:T(8,128)}), (f32[32,4480]{1,0:T(8,128)}, f32[32,4480]{1,0:T(8,128)})) %all-reduce.17.cloned.1.call-update) | async-done | bytes 1146896
  261.5 0.9 fusion.75
  262.3 0.9 divide_multiply_fusion.5
  263.6 4.2 multiply_reduce_fusion.2
  267.8 1.3 copy-done
  269.1 1.1 pad_maximum_fusion
  271.0 0.9 fusion.66
  272.0 0.9 fusion.67
  273.0 15.4 %all-gather.1 = bf16[16,3,2048]{2,1,0:T(4,128)(2,1)S(1)} all-gather(bf16[2,3,2048]{2,1,0:T(4,128)(2,1)S(1)} %copy.16), channel_id=3, replica_groups=mesh['tp'=4,'grp'=8] {'grp'}, dimensions={0}, use_global_device_ids=true | all-gather | bytes 221184 | tf_op jit(solution)/shard_map/all_gather | solution.py:75
  288.9 0.9 divide_multiply_fusion.3
  289.9 0.8 fusion.77
  291.0 61.5 %all-gather.8.cloned.1.call-done = bf16[16,32,64,128]{3,2,1,0:T(8,128)(2,1)} async-done(((bf16[2,32,64,128]{3,2,1,0:T(8,128)(2,1)}), bf16[16,32,64,128]{3,2,1,0:T(8,128)(2,1)}) %all-gather.8.cloned.1.call-update) | async-done | bytes 8388624 | tf_op jit(solution)/shard_map/all_gather | solution.py:74
  352.5 5.6 select_reduce_fusion
  358.1 0.9 slice_dynamic-update-slice_fusion
  359.0 2.8 multiply_reduce_fusion.1
  361.9 1.1 fusion.64
  363.0 14.0 %all-gather.4 = bf16[8,4,2048]{2,1,0:T(4,128)(2,1)S(1)} all-gather(bf16[1,4,2048]{2,1,0:T(4,128)(2,1)S(1)} %fusion.64), channel_id=1, replica_groups=mesh['tp'=4,'grp'=8] {'grp'}, dimensions={0}, use_global_device_ids=true | all-gather | bytes 147456 | tf_op jit(solution)/shard_map/all_gather | solution.py:119
  377.0 3.0 fusion.6
  380.0 18.5 %all-reduce.19 = bf16[32,1024]{1,0:T(8,128)(2,1)S(1)} all-reduce(f32[32,1024]{1,0:T(8,128)S(1)} %fusion.6), channel_id=1, replica_groups=mesh['tp'=4,'grp'=8] {'tp'}, use_global_device_ids=true, to_apply=%region_13.14 | all-reduce | flops 32768 | bytes 196608 | tf_op jit(solution)/shard_map/psum | solution.py:123
  398.7 8.3 %all_to_all.84 = bf16[8,4,1024]{2,1,0:T(4,128)(2,1)S(1)} all-to-all(bf16[8,4,1024]{2,1,0:T(4,128)(2,1)S(1)} %constant_dynamic-update-slice_fusion.16), channel_id=1, replica_groups=mesh['tp'=4,'grp'=8] {'grp'}, dimensions={0} | all-to-all | bytes 131072 | tf_op jit(solution)/shard_map/all_to_all | solution.py:139
  407.3 8.3 %all_to_all.85 = bf16[4,8,1024]{2,0,1:T(4,128)(2,1)S(1)} all-to-all(bf16[4,8,1024]{2,0,1:T(4,128)(2,1)S(1)} %multiply_convert_fusion), channel_id=1, replica_groups=mesh['tp'=4,'grp'=8] {'grp'}, dimensions={1} | all-to-all | bytes 131072 | tf_op jit(solution)/shard_map/all_to_all | solution.py:136
  415.9 5.1 fusion.85
  421.0 0.9 pad_maximum_fusion.4
  422.3 53.1 %all-reduce.15.cloned.1.call-done = f32[32,4480]{1,0:T(8,128)} async-done(((f32[32,4480]{1,0:T(8,128)}), f32[32,4480]{1,0:T(8,128)}) %all-reduce.15.cloned.1.call-update) | async-done | bytes 573456
  475.4 0.9 divide_multiply_fusion.1
  477.5 2.9 multiply_reduce_fusion
  480.4 1.0 fusion.63
  481.5 14.0 %all-gather.5 = bf16[8,4,2048]{2,1,0:T(4,128)(2,1)S(1)} all-gather(bf16[1,4,2048]{2,1,0:T(4,128)(2,1)S(1)} %get-tuple-element.64), channel_id=1, replica_groups=mesh['tp'=4,'grp'=8] {'grp'}, dimensions={0}, use_global_device_ids=true | all-gather | bytes 147456 | tf_op jit(solution)/shard_map/all_gather | solution.py:119
  495.5 3.0 fusion.2
  498.5 14.0 %all-gather.3 = bf16[8,4,2048]{2,1,0:T(4,128)(2,1)S(1)} all-gather(bf16[1,4,2048]{2,1,0:T(4,128)(2,1)S(1)} %get-tuple-element.63), channel_id=1, replica_groups=mesh['tp'=4,'grp'=8] {'grp'}, dimensions={0}, use_global_device_ids=true | all-gather | bytes 147456 | tf_op jit(solution)/shard_map/all_gather | solution.py:119
  512.5 3.0 fusion.4
  515.5 21.6 %all-reduce.20 = (bf16[32,1024]{1,0:T(8,128)(2,1)S(1)}, bf16[32,1024]{1,0:T(8,128)(2,1)S(1)}) all-reduce(f32[32,1024]{1,0:T(8,128)S(1)} %fusion.2, f32[32,1024]{1,0:T(8,128)S(1)} %fusion.4), channel_id=1, replica_groups=mesh['tp'=4,'grp'=8] {'tp'}, use_global_device_ids=true, to_apply=%region_17.18 | all-reduce | flops 65536 | bytes 393216 | tf_op jit(solution)/shard_map/psum | solution.py:123
  542.0 3.3 all-to-all-start.7
  550.1 1.1 all-to-all-done.7
  551.2 4.0 all-to-all-start.3
  555.2 5.9 %all-to-all-done.3 = bf16[8,4,1024]{2,1,0:T(4,128)(2,1)S(1)} async-done(((bf16[8,4,1024]{2,1,0:T(4,128)(2,1)}), bf16[8,4,1024]{2,1,0:T(4,128)(2,1)S(1)}, u32[]{:S(2)}, u32[]{:S(2)}) %all-to-all-start.3) | async-done | bytes 65568 | tf_op jit(solution)/shard_map/all_to_all | solution.py:139
  (158 shorter events, 25.5 us)
Async XLA Ops:
  10.4 47.1 %all-to-all-start.4 = ((bf16[4,8,1024]{2,0,1:T(4,128)(2,1)}), bf16[4,8,1024]{2,0,1:T(4,128)(2,1)S(1)}, u32[]{:S(2)}, u32[]{:S(2)}) async-start(bf16[4,8,1024]{2,0,1:T(4,128)(2,1)} %get-tuple-element.60), calls=%async_computation.4 | async-start | bytes 131072 | tf_op jit(solution)/shard_map/all_to_all | solution.py:136
  31.0 12.1 %copy-start.5 = (bf16[2,4,3,2048]{3,1,2,0:T(4,128)(2,1)S(1)}, bf16[2,4,3,2048]{3,1,2,0:T(4,128)(2,1)}, u32[]{:S(2)}) copy-start(bf16[2,4,3,2048]{3,1,2,0:T(4,128)(2,1)} %param.16) | copy-start | bytes 294916
  31.1 12.2 %copy-start.8 = (f32[2,4,2048]{2,1,0:T(4,128)S(1)}, f32[2,4,2048]{2,1,0:T(4,128)}, u32[]{:S(2)}) copy-start(f32[2,4,2048]{2,1,0:T(4,128)} %param.23) | copy-start | bytes 196612
  31.1 12.2 %copy-start.9 = (f32[2,2048]{1,0:T(2,128)S(1)}, f32[2,2048]{1,0:T(2,128)}, u32[]{:S(2)}) copy-start(f32[2,2048]{1,0:T(2,128)} %param.24) | copy-start | bytes 49156
  31.1 12.3 %copy-start.19 = (f32[2,32]{1,0:T(2,128)S(1)}, f32[2,32]{1,0:T(2,128)}, u32[]{:S(2)}) copy-start(f32[2,32]{1,0:T(2,128)} %param.22) | copy-start | bytes 772
  44.1 92.2 %copy-start.6 = (f32[2048]{0:T(1024)}, f32[2048]{0:T(1024)S(1)}, u32[]{:S(2)}) copy-start(f32[2048]{0:T(1024)S(1)} %mul.533) | copy-start | bytes 24580
  44.1 12.2 %copy-start.22 = (u32[32]{0:T(128)S(1)}, u32[32]{0:T(128)}, u32[]{:S(2)}) copy-start(u32[32]{0:T(128)} %constant.77) | copy-start | bytes 388
  44.1 18.8 %copy-start.20 = (f32[2,32]{1,0:T(2,128)S(1)}, f32[2,32]{1,0:T(2,128)}, u32[]{:S(2)}) copy-start(f32[2,32]{1,0:T(2,128)} %param.21) | copy-start | bytes 772
  44.1 18.8 %copy-start.21 = (f32[2,32]{1,0:T(2,128)S(1)}, f32[2,32]{1,0:T(2,128)}, u32[]{:S(2)}) copy-start(f32[2,32]{1,0:T(2,128)} %param.20) | copy-start | bytes 772
  44.1 24.5 %copy-start.2 = (bf16[2,1024,384]{2,1,0:T(8,128)(2,1)S(1)}, bf16[2,1024,384]{2,1,0:T(8,128)(2,1)}, u32[]{:S(2)}) copy-start(bf16[2,1024,384]{2,1,0:T(8,128)(2,1)} %param.19) | copy-start | bytes 4718596
  57.5 11.0 %all-to-all-start = ((bf16[4,8,1024]{2,0,1:T(4,128)(2,1)}), bf16[4,8,1024]{2,0,1:T(4,128)(2,1)S(1)}, u32[]{:S(2)}, u32[]{:S(2)}) async-start(bf16[4,8,1024]{2,0,1:T(4,128)(2,1)} %get-tuple-element.59), calls=%async_computation | async-start | bytes 131072 | tf_op jit(solution)/shard_map/all_to_all | solution.py:136
  62.6 67.3 %all-reduce.13.cloned.1.call-start = ((), (), s32[]{:S(2)}) async-start(), calls=%async_computation.9 | async-start | bytes 1146880
  63.5 68.4 %copy-start.14 = (f32[32]{0:T(128)}, f32[32]{0:T(128)S(1)}, u32[]{:S(2)}) copy-start(f32[32]{0:T(128)S(1)} %get-tuple-element.70) | copy-start | bytes 388
  63.5 68.4 %copy-start.16 = (f32[32]{0:T(128)}, f32[32]{0:T(128)S(1)}, u32[]{:S(2)}) copy-start(f32[32]{0:T(128)S(1)} %get-tuple-element.73) | copy-start | bytes 388
  136.2 51.4 %copy-start.4 = (bf16[2,4,8192]{2,1,0:T(4,128)(2,1)S(1)}, bf16[2,4,8192]{2,1,0:T(4,128)(2,1)}, u32[]{:S(2)}) copy-start(bf16[2,4,8192]{2,1,0:T(4,128)(2,1)} %param.14) | copy-start | bytes 393220
  178.4 9.2 %all-to-all-start.1 = ((bf16[8,4,1024]{2,1,0:T(4,128)(2,1)}), bf16[8,4,1024]{2,1,0:T(4,128)(2,1)S(1)}, u32[]{:S(2)}, u32[]{:S(2)}) async-start(bf16[8,4,1024]{2,1,0:T(4,128)(2,1)} %constant_dynamic-update-slice_fusion), calls=%async_computation.1 | async-start | bytes 131072 | tf_op jit(solution)/shard_map/all_to_all | solution.py:139
  188.5 9.2 %all-to-all-start.2 = ((bf16[4,8,1024]{2,0,1:T(4,128)(2,1)}), bf16[4,8,1024]{2,0,1:T(4,128)(2,1)S(1)}, u32[]{:S(2)}, u32[]{:S(2)}) async-start(bf16[4,8,1024]{2,0,1:T(4,128)(2,1)} %multiply_convert_fusion.2), calls=%async_computation.2 | async-start | bytes 131072 | tf_op jit(solution)/shard_map/all_to_all | solution.py:136
  191.9 69.6 %all-reduce.17.cloned.1.call-start = ((), (), s32[]{:S(2)}) async-start(), calls=%async_computation.11 | async-start | bytes 2293760
  199.1 64.2 %copy-start.10 = (f32[32]{0:T(128)S(1)}, f32[32]{0:T(128)}, u32[]{:S(2)}) copy-start(f32[32]{0:T(128)} %get-tuple-element.69) | copy-start | bytes 388
  199.1 64.2 %copy-start.12 = (f32[32]{0:T(128)S(1)}, f32[32]{0:T(128)}, u32[]{:S(2)}) copy-start(f32[32]{0:T(128)} %get-tuple-element.74) | copy-start | bytes 388
  204.9 147.5 %all-gather.8.cloned.1.call-start = ((), (), s32[]{:S(2)}) async-start(), calls=%async_computation.8 | async-start | bytes 9437184 | tf_op jit(solution)/shard_map/all_gather | solution.py:74
  263.5 27.2 %copy-start.15 = (f32[32]{0:T(128)S(1)}, f32[32]{0:T(128)}, u32[]{:S(2)}) copy-start(f32[32]{0:T(128)} %copy-done.14) | copy-start | bytes 388
  263.5 27.2 %copy-start.17 = (f32[32]{0:T(128)S(1)}, f32[32]{0:T(128)}, u32[]{:S(2)}) copy-start(f32[32]{0:T(128)} %copy-done.16) | copy-start | bytes 388
  267.8 1.3 copy-start
  270.2 205.2 %all-reduce.15.cloned.1.call-start = ((), (), s32[]{:S(2)}) async-start(), calls=%async_computation.10 | async-start | bytes 1146880
  358.1 3.8 copy-start.7
  361.8 53.8 %copy-start.3 = (bf16[2,1024,384]{2,1,0:T(8,128)(2,1)S(1)}, bf16[2,1024,384]{2,1,0:T(8,128)(2,1)}, u32[]{:S(2)}) copy-start(bf16[2,1024,384]{2,1,0:T(8,128)(2,1)} %param.19) | copy-start | bytes 4718596
  415.8 6.0 %copy-start.18 = (f32[32]{0:T(128)S(1)}, f32[32]{0:T(128)}, u32[]{:S(2)}) copy-start(f32[32]{0:T(128)} %get-tuple-element.65) | copy-start | bytes 388
  415.9 61.4 %copy-start.11 = (f32[32]{0:T(128)S(1)}, f32[32]{0:T(128)}, u32[]{:S(2)}) copy-start(f32[32]{0:T(128)} %get-tuple-element.69) | copy-start | bytes 388
  415.9 61.4 %copy-start.13 = (f32[32]{0:T(128)S(1)}, f32[32]{0:T(128)}, u32[]{:S(2)}) copy-start(f32[32]{0:T(128)} %get-tuple-element.74) | copy-start | bytes 388
  415.9 61.6 %copy-start.1 = (bf16[4,32,64,128]{3,2,1,0:T(8,128)(2,1)S(1)}, bf16[4,32,64,128]{3,2,1,0:T(8,128)(2,1)}, u32[]{:S(2)}) copy-start(bf16[4,32,64,128]{3,2,1,0:T(8,128)(2,1)} %get-tuple-element.31) | copy-start | bytes 6291460
  542.0 9.2 %all-to-all-start.7 = ((bf16[8,4,1024]{2,1,0:T(4,128)(2,1)}), bf16[8,4,1024]{2,1,0:T(4,128)(2,1)S(1)}, u32[]{:S(2)}, u32[]{:S(2)}) async-start(bf16[8,4,1024]{2,1,0:T(4,128)(2,1)} %constant_dynamic-update-slice_fusion.24), calls=%async_computation.7 | async-start | bytes 131072 | tf_op jit(solution)/shard_map/all_to_all | solution.py:139
  551.2 9.9 %all-to-all-start.3 = ((bf16[8,4,1024]{2,1,0:T(4,128)(2,1)}), bf16[8,4,1024]{2,1,0:T(4,128)(2,1)S(1)}, u32[]{:S(2)}, u32[]{:S(2)}) async-start(bf16[8,4,1024]{2,1,0:T(4,128)(2,1)} %constant_dynamic-update-slice_fusion.8), calls=%async_computation.3 | async-start | bytes 131072 | tf_op jit(solution)/shard_map/all_to_all | solution.py:139
Sparse Core Ops, SparseCore 0:
  74.7 55.1 all-reduce.12
  205.1 56.3 all-reduce.16
  270.4 82.0 all-gather.7
  422.0 53.4 all-reduce.14
